TPU v7x, 32 devices: a whole 2x2x4 slice. The times are simulated.
32 devices in a mesh: ctx: 8 (over y, x, core), head: 4 (over z).
Axes of the slice: x: 2, y: 2, z: 4, core: 2. Of those that a mesh axis runs over, the one named last changes fastest.
Arguments:
- tokens: bfloat16 [8192, 2048], P('ctx', 'head'), may hold values from -6 to 6
- w_query: bfloat16 [2048, 2048], P(None, 'head'), may hold values from -0.125 to 0.125
- w_value: bfloat16 [2048, 2048], P(None, 'head'), may hold values from -0.125 to 0.125
- w_out: bfloat16 [2048, 2048], P('head'), may hold values from -1.5 to 1.5
- doc_lengths: int32 [2], replicated, may hold values from 512 to 4096, as said below
Outputs:
- layer_out: bfloat16 [8192, 2048], P('ctx', 'head')
Inputs may be any that keep to these rules, and one draw needn't show every extreme that they name: `doc_lengths`: one of the two documents, drawn from the seed, has the full length 4096; the other has at least 512 valid tokens.
All inputs are finite; a program needn't handle non-finite values.
Results may differ from a plain program's by a relative error of at most 0.02.
Values may be sent and summed in bfloat16 or wider, within the bound.
A program may use at most 64 MiB of HBM per device.

v0:
```python
import jax
import jax.numpy as jnp
from jax import lax
from jax.sharding import PartitionSpec as P

HD = 128


score_bound = 24.0


def from_behind(value, axis, steps):
    count = lax.axis_size(axis)
    pairs = [(source, (source + steps) % count) for source in range(count)]
    return lax.ppermute(value, axis, pairs)


def unit_heads(projected, heads_here, head_size):
    shaped = projected.reshape(projected.shape[0], heads_here, head_size)
    scaled = shaped * lax.rsqrt(jnp.sum(shaped * shaped, axis=-1, keepdims=True) + 1e-06)
    return scaled.astype(jnp.bfloat16)


def per_device(tokens, w_query, w_value, w_out, doc_lengths):
    block_rows = tokens.shape[0]
    width_here = w_query.shape[1]
    heads_here = width_here // HD
    joined = jnp.concatenate([w_query, w_value], axis=1)
    projected = jnp.dot(
        lax.all_gather(tokens, "head", axis=1, tiled=True),
        joined,
        preferred_element_type=jnp.float32,
    )
    queries = unit_heads(projected[:, :width_here], heads_here, HD)
    own_values = projected[:, width_here:].astype(jnp.bfloat16).reshape(block_rows, heads_here, HD)
    ctx_count = lax.axis_size("ctx")
    ctx_here = lax.axis_index("ctx")
    doc_span = block_rows * ctx_count // 2
    own_first = ctx_here * block_rows

    def placement(start, length):
        position = start + jnp.arange(length, dtype=jnp.int32)
        doc_index = position // doc_span
        limit = jnp.where(doc_index == 0, doc_lengths[0], doc_lengths[1])
        return (position, doc_index, position - doc_index * doc_span < limit)

    own_position, own_doc, own_valid = placement(own_first, block_rows)

    def tile_weights(key_rows, key_start):
        key_position, key_doc, key_valid = placement(key_start, key_rows.shape[0])
        allowed = own_valid[:, None] & key_valid[None, :] & (own_doc[:, None] == key_doc[None, :])
        allowed = allowed & (own_position[:, None] != key_position[None, :])
        scores = (
            jnp.einsum("qhd,khd->hqk", queries, key_rows, preferred_element_type=jnp.float32)
            * score_bound
        )
        return jnp.exp(scores - score_bound) * allowed.astype(jnp.float32)[None]

    def own_update(key_rows, key_values, key_start, totals):
        weights_tile = tile_weights(key_rows, key_start)
        rounded = weights_tile.astype(jnp.bfloat16)
        numer = totals[0] + jnp.einsum(
            "hqk,khd->qhd", rounded, key_values, preferred_element_type=jnp.float32
        )
        return (numer, totals[1] + jnp.sum(weights_tile, axis=2))

    start_numer = jnp.zeros((block_rows, heads_here, HD), jnp.float32)
    start_denom = jnp.zeros((heads_here, block_rows), jnp.float32)
    numer, denom = own_update(queries, own_values, own_first, (start_numer, start_denom))
    moving_keys, moving_values = (queries, own_values)
    half_count = ctx_count // 2
    for distance in range(1, half_count + 1):
        moving_keys, moving_values = from_behind((moving_keys, moving_values), "ctx", 1)
        key_start = (ctx_here - distance) % ctx_count * block_rows
        if distance < half_count:

            def pair_update(
                totals, key_rows=moving_keys, key_values=moving_values, start_at=key_start
            ):
                weights_tile = tile_weights(key_rows, start_at)
                rounded = weights_tile.astype(jnp.bfloat16)
                numer_own = totals[0] + jnp.einsum(
                    "hqk,khd->qhd", rounded, key_values, preferred_element_type=jnp.float32
                )
                denom_own = totals[1] + jnp.sum(weights_tile, axis=2)
                numer_back = jnp.einsum(
                    "hqk,qhd->khd", rounded, own_values, preferred_element_type=jnp.float32
                )
                denom_back = jnp.sum(weights_tile, axis=1)
                return (numer_own, denom_own, numer_back, denom_back)

            numer, denom, numer_back, denom_back = pair_update(
                (numer, denom, start_numer, start_denom)
            )
            numer_back, denom_back = (
                from_behind(numer_back.astype(jnp.bfloat16), "ctx", -distance).astype(
                    numer_back.dtype
                ),
                from_behind(denom_back.astype(jnp.bfloat16), "ctx", -distance).astype(
                    denom_back.dtype
                ),
            )
            numer = numer + numer_back
            denom = denom + denom_back
        else:
            numer, denom = own_update(moving_keys, moving_values, key_start, (numer, denom))
    invalid = 1.0 - own_valid.astype(jnp.float32)
    attended = numer / (denom.T[:, :, None] + invalid[:, None, None])
    attended = attended.astype(jnp.bfloat16).reshape(block_rows, width_here)
    partial_out = jnp.dot(attended, w_out, preferred_element_type=jnp.float32)
    return lax.psum_scatter(
        partial_out.astype(jnp.bfloat16), "head", scatter_dimension=1, tiled=True
    )


def solution(mesh):
    return jax.shard_map(
        per_device,
        mesh=mesh,
        in_specs=(P("ctx", "head"), P(None, "head"), P(None, "head"), P("head", None), P()),
        out_specs=P("ctx", "head"),
        check_vma=False,
    )
```

profile of v0, /device:TPU:0, one launch (start us, length us, event | category | flops | bytes accessed | tf_op | source)
XLA Modules:
  0.0 348.3 jit_solution(1778041038881082832)
XLA Ops:
  12.5 9.7 %and_convert_fusion = (f32[1024,1024]{0,1:T(8,128)}, f32[1024,1024]{0,1:T(8,128)}, f32[1024,1024]{0,1:T(8,128)}, f32[1024,1024]{0,1:T(8,128)}, f32[1024,1024]{0,1:T(8,128)}) fusion(s32[1024]{0:T(1024)S(1)} %get-tuple-element.28, s32[1024]{0:T(1024)S(1)} %get-tuple-element.27, s32[1024]{0:T(1024)S(1)} %get-tuple-element.30, s32[1024]{0:T(1024)S(1)} %get-tuple-element.29, ...), kind=kLoop, calls=%fused_computation.27 | loop fusion | flops 31457280 | bytes 21017600 | tf_op jit(solution)/shard_map/convert_element_type | solution.py:57
  22.1 70.3 %all-gather.2.cloned.1.call-done = bf16[1024,2048]{1,0:T(8,128)(2,1)} async-done(((bf16[1024,512]{1,0:T(8,128)(2,1)}), bf16[1024,2048]{1,0:T(8,128)(2,1)}) %all-gather.2.cloned.1.call-update) | async-done | bytes 4194320 | tf_op jit(solution)/shard_map/all_gather | solution.py:30
  92.4 7.7 %fusion.24 = f32[1024,1024]{0,1:T(8,128)S(1)} fusion(bf16[1024,2048]{1,0:T(8,128)(2,1)} %all-gather.2.cloned.1.call-done, bf16[2048,512]{1,0:T(8,128)(2,1)} %param.7, bf16[2048,512]{1,0:T(8,128)(2,1)} %param.6), kind=kOutput, calls=%fused_computation.33 | convolution fusion | flops 4303355904 | bytes 12582912 | tf_op jit(solution)/shard_map/dot_general | solution.py:29
  103.0 2.9 copy.6
  105.9 2.8 multiply_convert_fusion
  110.2 5.7 %fusion = (f32[4,1024]{1,0:T(4,128)S(1)}, f32[4,1024,1024]{1,2,0:T(8,128)S(1)}) fusion(f32[1024,1024]{0,1:T(8,128)} %get-tuple-element.17, bf16[1024,4,128]{2,0,1:T(8,128)(2,1)} %multiply_convert_fusion), kind=kOutput, calls=%fused_computation.5 | convolution fusion | flops 1090514944 | bytes 22036480 | tf_op jit(solution)/shard_map/qhd,khd->hqk/dot_general | solution.py:54
  115.9 7.1 %fusion.6 = f32[4,128,1024]{2,1,0:T(8,128)} fusion(bf16[1024,4,128]{0,2,1:T(8,128)(2,1)} %bitcast.1, f32[4,1024,1024]{1,2,0:T(8,128)S(1)} %get-tuple-element.26, f32[1024,1024]{0,1:T(8,128)} %get-tuple-element.17), kind=kOutput, calls=%fused_computation.10 | convolution fusion | flops 1090519040 | bytes 24117248 | tf_op jit(solution)/shard_map/hqk,khd->qhd/dot_general | solution.py:62
  123.0 6.6 %collective-permute-done.1 = bf16[1024,4,128]{2,0,1:T(8,128)(2,1)} collective-permute-done((bf16[1024,4,128]{2,0,1:T(8,128)(2,1)}, bf16[1024,4,128]{2,0,1:T(8,128)(2,1)}, u32[]{:S(2)}, u32[]{:S(2)}) %collective-permute-start.1) | collective-permute-done | bytes 1048608 | tf_op jit(solution)/shard_map/ppermute | solution.py:15
  129.6 6.8 %fusion.76 = (f32[4,1024]{1,0:T(4,128)S(1)}, bf16[4,1024]{1,0:T(4,128)(2,1)S(1)}, bf16[4,1024,1024]{1,2,0:T(8,128)(2,1)S(1)}) fusion(f32[1024,1024]{0,1:T(8,128)} %get-tuple-element.16, bf16[1024,4,128]{2,0,1:T(8,128)(2,1)} %multiply_convert_fusion, bf16[1024,4,128]{2,0,1:T(8,128)(2,1)} %collective-permute-done.1), kind=kOutput, calls=%fused_computation.113 | convolution fusion | flops 1098899456 | bytes 14704640 | tf_op jit(solution)/shard_map/qhd,khd->hqk/dot_general | solution.py:54
  136.5 5.1 %fusion.48 = bf16[1024,4,128]{0,2,1:T(8,128)(2,1)} fusion(bf16[1024,4,128]{0,2,1:T(8,128)(2,1)} %bitcast.1, bf16[4,1024,1024]{1,2,0:T(8,128)(2,1)S(1)} %get-tuple-element.24), kind=kOutput, calls=%fused_computation.50 | convolution fusion | flops 1074266112 | bytes 10485760 | tf_op jit(solution)/shard_map/hqk,qhd->khd/dot_general | solution.py:86
  141.6 2.6 collective-permute-start.2
  147.3 6.1 %fusion.77 = (f32[4,1024]{1,0:T(4,128)S(1)}, bf16[4,1024]{1,0:T(4,128)(2,1)S(1)}, bf16[4,1024,1024]{1,2,0:T(8,128)(2,1)S(1)}) fusion(f32[1024,1024]{0,1:T(8,128)S(1)} %copy-done.4, bf16[1024,4,128]{2,0,1:T(8,128)(2,1)} %multiply_convert_fusion, bf16[1024,4,128]{2,0,1:T(8,128)(2,1)S(1)} %collective-permute-done.4), kind=kOutput, calls=%fused_computation.114 | convolution fusion | flops 1098899456 | bytes 14704640 | tf_op jit(solution)/shard_map/qhd,khd->hqk/dot_general | solution.py:54
  155.8 13.4 %collective-permute-done.3 = bf16[1024,4,128]{0,2,1:T(8,128)(2,1)S(1)} collective-permute-done((bf16[1024,4,128]{0,2,1:T(8,128)(2,1)}, bf16[1024,4,128]{0,2,1:T(8,128)(2,1)S(1)}, u32[]{:S(2)}, u32[]{:S(2)}) %collective-permute-start.3) | collective-permute-done | bytes 1048608 | tf_op jit(solution)/shard_map/ppermute | solution.py:15
  169.2 5.1 %fusion.45 = bf16[1024,4,128]{0,2,1:T(8,128)(2,1)} fusion(bf16[1024,4,128]{0,2,1:T(8,128)(2,1)} %bitcast.1, bf16[4,1024,1024]{1,2,0:T(8,128)(2,1)S(1)} %get-tuple-element.23), kind=kOutput, calls=%fused_computation.49 | convolution fusion | flops 1074266112 | bytes 10485760 | tf_op jit(solution)/shard_map/hqk,qhd->khd/dot_general | solution.py:86
  175.5 5.1 %collective-permute-done.7 = bf16[1024,4,128]{2,0,1:T(8,128)(2,1)} collective-permute-done((bf16[1024,4,128]{2,0,1:T(8,128)(2,1)S(1)}, bf16[1024,4,128]{2,0,1:T(8,128)(2,1)}, u32[]{:S(2)}, u32[]{:S(2)}) %collective-permute-start.7) | collective-permute-done | bytes 1048608 | tf_op jit(solution)/shard_map/ppermute | solution.py:15
  180.6 6.2 %fusion.78 = (f32[4,1024]{1,0:T(4,128)S(1)}, bf16[4,1024]{1,0:T(4,128)(2,1)S(1)}, bf16[4,1024,1024]{1,2,0:T(8,128)(2,1)S(1)}) fusion(f32[1024,1024]{0,1:T(8,128)S(1)} %copy-done.3, bf16[1024,4,128]{2,0,1:T(8,128)(2,1)} %multiply_convert_fusion, bf16[1024,4,128]{2,0,1:T(8,128)(2,1)} %collective-permute-done.7), kind=kOutput, calls=%fused_computation.115 | convolution fusion | flops 1098899456 | bytes 14704640 | tf_op jit(solution)/shard_map/qhd,khd->hqk/dot_general | solution.py:54
  186.8 4.1 %fusion.42 = bf16[1024,4,128]{0,2,1:T(8,128)(2,1)S(1)} fusion(bf16[1024,4,128]{0,2,1:T(8,128)(2,1)} %bitcast.1, bf16[4,1024,1024]{1,2,0:T(8,128)(2,1)S(1)} %get-tuple-element.22), kind=kOutput, calls=%fused_computation.48 | convolution fusion | flops 1074266112 | bytes 10485760 | tf_op jit(solution)/shard_map/hqk,qhd->khd/dot_general | solution.py:86
  193.9 3.8 %fusion.14 = f32[4,128,1024]{2,1,0:T(8,128)} fusion(bf16[1024,4,128]{0,2,1:T(8,128)(2,1)} %collective-permute-done.6, bf16[4,1024,1024]{1,2,0:T(8,128)(2,1)S(1)} %get-tuple-element.22), kind=kOutput, calls=%fused_computation.17 | convolution fusion | flops 1073741824 | bytes 11534336 | tf_op jit(solution)/shard_map/hqk,khd->qhd/dot_general | solution.py:82
  197.7 13.3 %collective-permute-done.10 = bf16[1024,4,128]{2,0,1:T(8,128)(2,1)S(1)} collective-permute-done((bf16[1024,4,128]{2,0,1:T(8,128)(2,1)}, bf16[1024,4,128]{2,0,1:T(8,128)(2,1)S(1)}, u32[]{:S(2)}, u32[]{:S(2)}) %collective-permute-start.10) | collective-permute-done | bytes 1048608 | tf_op jit(solution)/shard_map/ppermute | solution.py:15
  212.0 9.1 %fusion.2 = (f32[4,1024]{1,0:T(4,128)S(1)}, f32[4,1024,1024]{1,2,0:T(8,128)}) fusion(f32[1024,1024]{0,1:T(8,128)S(1)} %copy-done.1, bf16[1024,4,128]{2,0,1:T(8,128)(2,1)} %multiply_convert_fusion, bf16[1024,4,128]{2,0,1:T(8,128)(2,1)} %copy-done.7), kind=kOutput, calls=%fused_computation.7 | convolution fusion | flops 1090514944 | bytes 23085056 | tf_op jit(solution)/shard_map/qhd,khd->hqk/dot_general | solution.py:54
  221.0 26.1 %collective-permute-done.13 = bf16[4,1024]{1,0:T(4,128)(2,1)S(1)} collective-permute-done((bf16[4,1024]{1,0:T(4,128)(2,1)S(1)}, bf16[4,1024]{1,0:T(4,128)(2,1)S(1)}, u32[]{:S(2)}, u32[]{:S(2)}) %collective-permute-start.13) | collective-permute-done | bytes 8224 | tf_op jit(solution)/shard_map/ppermute | solution.py:15
  249.1 10.5 %fusion.28 = bf16[1024,4,128]{0,2,1:T(8,128)(2,1)} fusion(f32[4,128,1024]{2,1,0:T(8,128)} %fusion.14, f32[4,128,1024]{2,1,0:T(8,128)S(1)} %fusion.18, bf16[1024,4,128]{0,2,1:T(8,128)(2,1)} %copy-done.5, bf16[1024,4,128]{0,2,1:T(8,128)(2,1)} %collective-permute-done.5, bf16[1024,4,128]{0,2,1:T(8,128)(2,1)} %collective-permute-done.2, ...), kind=kOutput, calls=%fused_computation.37 | convolution fusion | flops 1096810496 | bytes 34619392 | tf_op jit(solution)/shard_map/hqk,khd->qhd/dot_general | solution.py:62
  259.6 5.6 %convolution_convert_fusion = bf16[1024,2048]{1,0:T(8,128)(2,1)} fusion(bf16[1024,512]{0,1:T(8,128)(2,1)} %bitcast.66, bf16[512,2048]{1,0:T(8,128)(2,1)S(1)} %copy-done), kind=kOutput, calls=%fused_computation.32 | convolution fusion | flops 2149580800 | bytes 7340032 | tf_op jit(solution)/shard_map/dot_general | solution.py:110
  265.2 76.2 %reduce-scatter.2.cloned.1.call-done = bf16[1024,512]{1,0:T(8,128)(2,1)} async-done(((bf16[1024,2048]{1,0:T(8,128)(2,1)}), bf16[1024,512]{1,0:T(8,128)(2,1)}) %reduce-scatter.2.cloned.1.call-update) | async-done | bytes 1048592 | tf_op jit(solution)/shard_map/reduce_scatter | solution.py:111
  (58 shorter events, 22.9 us)
Async XLA Ops:
  6.5 253.1 %copy-start = (bf16[512,2048]{1,0:T(8,128)(2,1)S(1)}, bf16[512,2048]{1,0:T(8,128)(2,1)}, u32[]{:S(2)}) copy-start(bf16[512,2048]{1,0:T(8,128)(2,1)} %param.8) | copy-start | bytes 6291460
  6.5 85.9 %all-gather.2.cloned.1.call-start = ((), (), s32[]{:S(2)}) async-start(), calls=%async_computation.1 | async-start | bytes 5242880 | tf_op jit(solution)/shard_map/all_gather | solution.py:30
  7.3 334.2 %reduce-scatter.2.cloned.1.call-start = ((), (), s32[]{:S(2)}) async-start(), calls=%async_computation.2 | async-start | bytes 5242880 | tf_op jit(solution)/shard_map/reduce_scatter | solution.py:111
  102.9 41.4 %collective-permute-start = (bf16[1024,4,128]{0,2,1:T(8,128)(2,1)}, bf16[1024,4,128]{0,2,1:T(8,128)(2,1)}, u32[]{:S(2)}, u32[]{:S(2)}) collective-permute-start(bf16[1024,4,128]{0,2,1:T(8,128)(2,1)} %bitcast.1), channel_id=1, source_target_pairs={{0,4},{4,8},{8,12},{12,16},{16,20},{20,24},{24,28},{28,0},{1,5},{5... | collective-permute-start | bytes 3145736 | tf_op jit(solution)/shard_map/ppermute | solution.py:15
  108.7 21.0 %collective-permute-start.1 = (bf16[1024,4,128]{2,0,1:T(8,128)(2,1)}, bf16[1024,4,128]{2,0,1:T(8,128)(2,1)}, u32[]{:S(2)}, u32[]{:S(2)}) collective-permute-start(bf16[1024,4,128]{2,0,1:T(8,128)(2,1)} %multiply_convert_fusion), channel_id=1, source_target_pairs={{0,4},{4,8},{8,12},{12,16},{16,20},{20,24},{24,28},{28,0},{1,5},{5... | collective-permute-start | bytes 3145736 | tf_op jit(solution)/shard_map/ppermute | solution.py:15
  129.6 17.6 %collective-permute-start.4 = (bf16[1024,4,128]{2,0,1:T(8,128)(2,1)}, bf16[1024,4,128]{2,0,1:T(8,128)(2,1)S(1)}, u32[]{:S(2)}, u32[]{:S(2)}) collective-permute-start(bf16[1024,4,128]{2,0,1:T(8,128)(2,1)} %collective-permute-done.1), channel_id=1, source_target_pairs={{0,4},{4,8},{8,12},{12,16},{16,20},{20,24},{24,28},{28,0},{1,5},{5... | collective-permute-start | bytes 3145736 | tf_op jit(solution)/shard_map/ppermute | solution.py:15
  141.6 5.7 %copy-start.4 = (f32[1024,1024]{0,1:T(8,128)S(1)}, f32[1024,1024]{0,1:T(8,128)}, u32[]{:S(2)}) copy-start(f32[1024,1024]{0,1:T(8,128)} %get-tuple-element.15) | copy-start | bytes 12582916
  141.6 105.5 %collective-permute-start.2 = (bf16[1024,4,128]{0,2,1:T(8,128)(2,1)}, bf16[1024,4,128]{0,2,1:T(8,128)(2,1)}, u32[]{:S(2)}, u32[]{:S(2)}) collective-permute-start(bf16[1024,4,128]{0,2,1:T(8,128)(2,1)} %fusion.48), channel_id=1, source_target_pairs={{0,28},{4,0},{8,4},{12,8},{16,12},{20,16},{24,20},{28,24},{1,29},{... | collective-permute-start | bytes 3145736 | tf_op jit(solution)/shard_map/ppermute | solution.py:15
  144.2 46.7 %collective-permute-start.11 = (bf16[4,1024]{1,0:T(4,128)(2,1)S(1)}, bf16[4,1024]{1,0:T(4,128)(2,1)S(1)}, u32[]{:S(2)}, u32[]{:S(2)}) collective-permute-start(bf16[4,1024]{1,0:T(4,128)(2,1)S(1)} %get-tuple-element.6), channel_id=1, source_target_pairs={{0,28},{4,0},{8,4},{12,8},{16,12},{20,16},{24,20},{28,24},{1,29},{... | collective-permute-start | bytes 24584 | tf_op jit(solution)/shard_map/ppermute | solution.py:15
  144.3 24.9 %collective-permute-start.3 = (bf16[1024,4,128]{0,2,1:T(8,128)(2,1)}, bf16[1024,4,128]{0,2,1:T(8,128)(2,1)S(1)}, u32[]{:S(2)}, u32[]{:S(2)}) collective-permute-start(bf16[1024,4,128]{0,2,1:T(8,128)(2,1)} %collective-permute-done), channel_id=1, source_target_pairs={{0,4},{4,8},{8,12},{12,16},{16,20},{20,24},{24,28},{28,0},{1,5},{5... | collective-permute-start | bytes 3145736 | tf_op jit(solution)/shard_map/ppermute | solution.py:15
  153.4 39.8 %collective-permute-start.12 = (bf16[4,1024]{1,0:T(4,128)(2,1)S(1)}, bf16[4,1024]{1,0:T(4,128)(2,1)S(1)}, u32[]{:S(2)}, u32[]{:S(2)}) collective-permute-start(bf16[4,1024]{1,0:T(4,128)(2,1)S(1)} %get-tuple-element.8), channel_id=1, source_target_pairs={{0,24},{4,28},{8,0},{12,4},{16,8},{20,12},{24,16},{28,20},{1,25},{... | collective-permute-start | bytes 24584 | tf_op jit(solution)/shard_map/ppermute | solution.py:15
  154.0 26.6 %collective-permute-start.7 = (bf16[1024,4,128]{2,0,1:T(8,128)(2,1)S(1)}, bf16[1024,4,128]{2,0,1:T(8,128)(2,1)}, u32[]{:S(2)}, u32[]{:S(2)}) collective-permute-start(bf16[1024,4,128]{2,0,1:T(8,128)(2,1)S(1)} %collective-permute-done.4), channel_id=1, source_target_pairs={{0,4},{4,8},{8,12},{12,16},{16,20},{20,24},{24,28},{28,0},{1,5},{5... | collective-permute-start | bytes 3145736 | tf_op jit(solution)/shard_map/ppermute | solution.py:15
  169.2 24.7 %collective-permute-start.6 = (bf16[1024,4,128]{0,2,1:T(8,128)(2,1)S(1)}, bf16[1024,4,128]{0,2,1:T(8,128)(2,1)}, u32[]{:S(2)}, u32[]{:S(2)}) collective-permute-start(bf16[1024,4,128]{0,2,1:T(8,128)(2,1)S(1)} %collective-permute-done.3), channel_id=1, source_target_pairs={{0,4},{4,8},{8,12},{12,16},{16,20},{20,24},{24,28},{28,0},{1,5},{5... | collective-permute-start | bytes 3145736 | tf_op jit(solution)/shard_map/ppermute | solution.py:15
  174.3 6.3 %copy-start.3 = (f32[1024,1024]{0,1:T(8,128)S(1)}, f32[1024,1024]{0,1:T(8,128)}, u32[]{:S(2)}) copy-start(f32[1024,1024]{0,1:T(8,128)} %get-tuple-element.14) | copy-start | bytes 12582916
  180.6 30.4 %collective-permute-start.10 = (bf16[1024,4,128]{2,0,1:T(8,128)(2,1)}, bf16[1024,4,128]{2,0,1:T(8,128)(2,1)S(1)}, u32[]{:S(2)}, u32[]{:S(2)}) collective-permute-start(bf16[1024,4,128]{2,0,1:T(8,128)(2,1)} %collective-permute-done.7), channel_id=1, source_target_pairs={{0,4},{4,8},{8,12},{12,16},{16,20},{20,24},{24,28},{28,0},{1,5},{5... | collective-permute-start | bytes 3145736 | tf_op jit(solution)/shard_map/ppermute | solution.py:15
  190.9 21.1 %copy-start.1 = (f32[1024,1024]{0,1:T(8,128)S(1)}, f32[1024,1024]{0,1:T(8,128)}, u32[]{:S(2)}) copy-start(f32[1024,1024]{0,1:T(8,128)} %get-tuple-element.13) | copy-start | bytes 12582916
  190.9 56.2 %collective-permute-start.5 = (bf16[1024,4,128]{0,2,1:T(8,128)(2,1)}, bf16[1024,4,128]{0,2,1:T(8,128)(2,1)}, u32[]{:S(2)}, u32[]{:S(2)}) collective-permute-start(bf16[1024,4,128]{0,2,1:T(8,128)(2,1)} %fusion.45), channel_id=1, source_target_pairs={{0,24},{4,28},{8,0},{12,4},{16,8},{20,12},{24,16},{28,20},{1,25},{... | collective-permute-start | bytes 3145736 | tf_op jit(solution)/shard_map/ppermute | solution.py:15
  193.2 53.9 %collective-permute-start.8 = (bf16[1024,4,128]{0,2,1:T(8,128)(2,1)S(1)}, bf16[1024,4,128]{0,2,1:T(8,128)(2,1)S(1)}, u32[]{:S(2)}, u32[]{:S(2)}) collective-permute-start(bf16[1024,4,128]{0,2,1:T(8,128)(2,1)S(1)} %fusion.42), channel_id=1, source_target_pairs={{0,20},{4,24},{8,28},{12,0},{16,4},{20,8},{24,12},{28,16},{1,21},{... | collective-permute-start | bytes 3145736 | tf_op jit(solution)/shard_map/ppermute | solution.py:15
  193.9 54.2 %collective-permute-start.9 = (bf16[1024,4,128]{0,2,1:T(8,128)(2,1)}, bf16[1024,4,128]{0,2,1:T(8,128)(2,1)S(1)}, u32[]{:S(2)}, u32[]{:S(2)}) collective-permute-start(bf16[1024,4,128]{0,2,1:T(8,128)(2,1)} %collective-permute-done.6), channel_id=1, source_target_pairs={{0,4},{4,8},{8,12},{12,16},{16,20},{20,24},{24,28},{28,0},{1,5},{5... | collective-permute-start | bytes 3145736 | tf_op jit(solution)/shard_map/ppermute | solution.py:15
  211.0 1.0 copy-start.7
  211.0 36.1 %collective-permute-start.13 = (bf16[4,1024]{1,0:T(4,128)(2,1)S(1)}, bf16[4,1024]{1,0:T(4,128)(2,1)S(1)}, u32[]{:S(2)}, u32[]{:S(2)}) collective-permute-start(bf16[4,1024]{1,0:T(4,128)(2,1)S(1)} %get-tuple-element.10), channel_id=1, source_target_pairs={{0,20},{4,24},{8,28},{12,0},{16,4},{20,8},{24,12},{28,16},{1,21},{... | collective-permute-start | bytes 24584 | tf_op jit(solution)/shard_map/ppermute | solution.py:15
  212.0 37.1 %copy-start.2 = (f32[4,128,1024]{2,1,0:T(8,128)S(1)}, f32[4,128,1024]{2,1,0:T(8,128)}, u32[]{:S(2)}) copy-start(f32[4,128,1024]{2,1,0:T(8,128)} %fusion.6) | copy-start | bytes 6291460
  247.1 1.0 copy-start.5
  248.1 1.0 copy-start.6
Sparse Core Ops, SparseCore 0:
  8.9 83.4 all-gather.1
  265.3 76.0 reduce-scatter.1
where the time goes:
time: 349 us; the launch traced here: 348 us
  waiting for transfers between devices  212 us (61%)
  matrix products  86.6 us (25%)
  other arithmetic  16.4 us (5%)
  between operations  13.7 us (4%)
  starting transfers between devices  10.4 us (3%)
  local copies, waits for them, and re-layouts  9.52 us (3%)
    reduce_scatter x1, waiting for transfers between devices, per_device(): lax.psum_scatter(partial_out.astype(jnp.bfloat16), 'head', scatter_dimens...  76.2 us
    all_gather x1, waiting for transfers between devices, per_device(): lax.all_gather(tokens, 'head', axis=1, tiled=True)  70.3 us
    ppermute x14, waiting for transfers between devices, from_behind(): return lax.ppermute(value, axis, pairs)  64.4 us
    dot_general x5, matrix products, tile_weights(): jnp.einsum('qhd,khd->hqk', queries, key_rows, preferred_element_type=jnp....  33.9 us
    dot_general x2, matrix products, own_update(): jnp.einsum('hqk,khd->qhd', rounded, key_values, preferred_element_type=jn...  17.6 us
    dot_general x3, matrix products, pair_update(): jnp.einsum('hqk,qhd->khd', rounded, own_values, preferred_element_type=jn...  14.3 us
    ppermute x14, starting transfers between devices, from_behind(): return lax.ppermute(value, axis, pairs)  10.4 us
    convert_element_type x1, other arithmetic, tile_weights(): return jnp.exp(scores - score_bound) * allowed.astype(jnp.float32)[None]  9.66 us
  transfers between devices with their start and end apart: 16, of which 7 were waited for; matrix products, arithmetic and copies ran while one was open for 24% of the time, Pallas kernels for 0%

commit v1 on v0

v1 whole, which is shorter than its diff:
```python
import functools
import math

import jax
import jax.numpy as jnp
from jax import lax
from jax.experimental import pallas as pl
from jax.experimental.pallas import tpu as pltpu
from jax.sharding import PartitionSpec as P

HD = 128
SCORE_BOUND = 24.0
EXP2_SCALE = SCORE_BOUND * math.log2(math.e)
GATHER_CHUNKS = 8
QUERY_CHUNKS = 4
MESH = pl.DeviceIdType.MESH


def layer_kernel(
    n, g, tok_hbm, wq_hbm, wv_hbm, wo_hbm, lengths, out_ref,
    tok, w, wo, q, kv, ones, att, from_low, from_high, outgoing, own_sum,
    load_sem, up_send, down_send, tok_recv, kv_send, kv_pass, kv_recv,
    sum_send, low_recv, high_recv,
):
    rows, wide = tok_hbm.shape
    heads = wide // HD
    half = g // 2
    gather_chunks, query_chunks = GATHER_CHUNKS, QUERY_CHUNKS
    step_rows = rows // gather_chunks
    query_rows = rows // query_chunks
    k = lax.axis_index("head")
    ctx = lax.axis_index("ctx")
    doc = ctx // g
    base = doc * g
    j = ctx - base
    partner = j + 1 - 2 * lax.rem(j, 2)

    loads = [
        pltpu.make_async_copy(tok_hbm, tok.at[k], load_sem.at[0]),
        pltpu.make_async_copy(wq_hbm, w.at[:, pl.ds(0, wide)], load_sem.at[1]),
        pltpu.make_async_copy(wv_hbm, w.at[:, pl.ds(wide, wide)], load_sem.at[2]),
        pltpu.make_async_copy(wo_hbm, wo, load_sem.at[3]),
    ]
    for load in loads:
        load.start()

    barrier = pltpu.get_barrier_semaphore()

    def greet(where):
        pl.semaphore_signal(barrier, inc=1, device_id=where, device_id_type=MESH)

    @pl.when(k > 0)
    def _():
        greet({"head": k - 1})

    @pl.when(k < n - 1)
    def _():
        greet({"head": k + 1})

    greet({"ctx": base + partner})
    for m in range(1, half):
        greet({"ctx": base + lax.rem(j + 2 * m, g)})
    pl.semaphore_wait(
        barrier, jnp.where(k > 0, 1, 0) + jnp.where(k < n - 1, 1, 0) + half
    )

    limit = jnp.where(doc == 0, lengths[0], lengths[1])

    def valid_rows(first, count):
        position = first + lax.broadcasted_iota(jnp.int32, (count, HD), 0)
        return jnp.where(position < limit, 1.0, 0.0)

    def chunk(c):
        return pl.ds(pl.multiple_of(c * step_rows, step_rows), step_rows)

    def tok_copy(source, c, to, sends):
        piece = tok.at[source, chunk(c)]
        return pltpu.make_async_remote_copy(
            src_ref=piece, dst_ref=piece, send_sem=sends.at[source, c],
            recv_sem=tok_recv.at[source, c], device_id={"head": to}, device_id_type=MESH,
        )

    def send_tok(source, c, up):
        if up:
            @pl.when(k < n - 1)
            def _():
                tok_copy(source, c, k + 1, up_send).start()
        else:
            @pl.when(k > 0)
            def _():
                tok_copy(source, c, k - 1, down_send).start()

    def arrive(source, c, up):
        tok_copy(source, c, k, up_send).wait_recv()
        send_tok(source, c, up)

    def kv_copy(slot, c, to, sem):
        piece = kv.at[slot, chunk(c)]
        return pltpu.make_async_remote_copy(
            src_ref=piece, dst_ref=piece, send_sem=sem, recv_sem=kv_recv.at[slot, c],
            device_id={"ctx": base + to}, device_id_type=MESH,
        )

    def behind(m):
        return lax.rem(j + g - 2 * m, g)

    def pass_on(c):
        for m in range(1, half):
            slot = behind(m)
            kv_copy(slot, c, partner, kv_pass.at[m, c]).wait_recv()
            kv_copy(slot, c, partner, kv_pass.at[m, c]).start()

    loads[0].wait()
    send_tok(k, 0, True)
    send_tok(k, 0, False)
    ones[...] = jnp.concatenate(
        [valid_rows(block * rows, rows) for block in range(g)], axis=0
    ).astype(jnp.bfloat16)
    loads[1].wait()
    loads[2].wait()

    def gather_step(c, carry):
        for distance in range(1, n):
            @pl.when(k - distance >= 0)
            def _():
                arrive(k - distance, c, True)

            @pl.when(k + distance < n)
            def _():
                arrive(k + distance, c, False)

        @pl.when(c + 1 < gather_chunks)
        def _():
            send_tok(k, c + 1, True)
            send_tok(k, c + 1, False)

        total = jnp.dot(tok[0, chunk(c)], w[0:wide], preferred_element_type=jnp.float32)
        for s in range(1, n):
            total += jnp.dot(
                tok[s, chunk(c)], w[s * wide:(s + 1) * wide],
                preferred_element_type=jnp.float32,
            )
        valid = valid_rows(j * rows + c * step_rows, step_rows)
        for h in range(heads):
            columns = slice(h * HD, (h + 1) * HD)
            part = total[:, columns]
            unit = part * lax.rsqrt(jnp.sum(part * part, axis=1, keepdims=True) + 1e-06)
            kv[j, chunk(c), columns] = unit.astype(jnp.bfloat16)
            q[chunk(c), columns] = (unit * EXP2_SCALE).astype(jnp.bfloat16)
            shifted = slice(wide + h * HD, wide + (h + 1) * HD)
            kv[j, chunk(c), shifted] = (total[:, shifted] * valid).astype(jnp.bfloat16)
        for m in range(1, half):
            kv_copy(j, c, lax.rem(j + 2 * m, g), kv_send.at[m, c]).start()
        kv_copy(j, c, partner, kv_send.at[0, c]).start()

        @pl.when(c > 0)
        def _():
            pass_on(c - 1)

        return carry

    lax.fori_loop(0, gather_chunks, gather_step, 0)
    pass_on(gather_chunks - 1)
    loads[3].wait()

    def gather_end(c, carry):
        kv_copy(partner, c, partner, kv_send.at[0, c]).wait_recv()
        for m in range(1, half):
            slot = lax.rem(partner + g - 2 * m, g)
            kv_copy(slot, c, partner, kv_pass.at[m, c]).wait_recv()
        return carry

    lax.fori_loop(0, gather_chunks, gather_end, 0)

    def sum_copy(c, d, to, landing, recv):
        return pltpu.make_async_remote_copy(
            src_ref=outgoing.at[c, d], dst_ref=landing.at[c, d], send_sem=sum_send.at[c, d],
            recv_sem=recv.at[c, d], device_id={"head": to}, device_id_type=MESH,
        )

    def query_chunk(c):
        return pl.ds(pl.multiple_of(c * query_rows, query_rows), query_rows)

    def share(d):
        columns = pl.ds(pl.multiple_of(d * wide, HD), wide)
        return jnp.dot(att[...], wo[:, columns], preferred_element_type=jnp.float32)

    def query_step(c, carry):
        own = c * query_rows
        valid = valid_rows(j * rows + own, query_rows)
        row = lax.broadcasted_iota(jnp.int32, (query_rows, rows), 0) + own
        column = lax.broadcasted_iota(jnp.int32, (query_rows, rows), 1)
        for h in range(heads):
            columns = slice(h * HD, (h + 1) * HD)
            shifted = slice(wide + h * HD, wide + (h + 1) * HD)
            queries = q[query_chunk(c), columns]
            total = None
            for b in range(g):
                block = lax.rem(j + b, g)
                scores = lax.dot_general(
                    queries, kv[block, :, columns], (((1,), (1,)), ((), ())),
                    preferred_element_type=jnp.float32,
                )
                weights = jnp.exp2(scores)
                if b == 0:
                    weights = jnp.where(row != column, weights, 0.0)
                block_rows = pl.ds(pl.multiple_of(block * rows, rows), rows)
                values = jnp.concatenate(
                    [kv[block, :, shifted], ones[block_rows]], axis=1
                )
                term = jnp.dot(
                    weights.astype(jnp.bfloat16), values, preferred_element_type=jnp.float32
                )
                total = term if total is None else total + term
            result = valid * total[:, :HD] / (total[:, HD:] + (1.0 - valid))
            att[:, columns] = result.astype(jnp.bfloat16)

        def emit(d, to, waits, landing, recv):
            @pl.when(waits)
            def _():
                sum_copy(c, d, k, landing, recv).wait_recv()
                outgoing[c, d] = (share(d) + landing[c, d].astype(jnp.float32)).astype(
                    jnp.bfloat16
                )

            @pl.when(jnp.logical_not(waits))
            def _():
                outgoing[c, d] = share(d).astype(jnp.bfloat16)

            sum_copy(c, d, to, landing, recv).start()

        for off in range(n - 1, 0, -1):
            @pl.when(k + off < n)
            def _():
                emit(k + off, k + 1, k > 0, from_low, low_recv)

            @pl.when(k - off >= 0)
            def _():
                emit(k - off, k - 1, k < n - 1, from_high, high_recv)

        own_sum[query_chunk(c)] = share(k)
        return carry

    lax.fori_loop(0, query_chunks, query_step, 0)

    def finish(c, carry):
        @pl.when(k > 0)
        def _():
            sum_copy(c, k, k, from_low, low_recv).wait_recv()
            own_sum[query_chunk(c)] += from_low[c, k].astype(jnp.float32)

        @pl.when(k < n - 1)
        def _():
            sum_copy(c, k, k, from_high, high_recv).wait_recv()
            own_sum[query_chunk(c)] += from_high[c, k].astype(jnp.float32)

        out_ref[query_chunk(c)] = own_sum[query_chunk(c)].astype(out_ref.dtype)
        return carry

    lax.fori_loop(0, query_chunks, finish, 0)

    def drain_gather(c, carry):
        for s in range(n):
            @pl.when(jnp.logical_and(s <= k, k < n - 1))
            def _():
                tok_copy(s, c, k + 1, up_send).wait_send()

            @pl.when(jnp.logical_and(s >= k, k > 0))
            def _():
                tok_copy(s, c, k - 1, down_send).wait_send()

        kv_copy(j, c, partner, kv_send.at[0, c]).wait_send()
        for m in range(1, half):
            kv_copy(j, c, partner, kv_send.at[m, c]).wait_send()
            kv_copy(behind(m), c, partner, kv_pass.at[m, c]).wait_send()
        return carry

    lax.fori_loop(0, gather_chunks, drain_gather, 0)

    def drain_sums(c, carry):
        for d in range(n):
            @pl.when(d > k)
            def _():
                sum_copy(c, d, k + 1, from_low, low_recv).wait_send()

            @pl.when(d < k)
            def _():
                sum_copy(c, d, k - 1, from_high, high_recv).wait_send()

        return carry

    lax.fori_loop(0, query_chunks, drain_sums, 0)


def per_device(tokens, w_query, w_value, w_out, doc_lengths):
    n = lax.axis_size("head")
    g = lax.axis_size("ctx") // 2
    rows, wide = tokens.shape
    depth = w_query.shape[0]
    query_rows = rows // QUERY_CHUNKS
    bf16, f32 = jnp.bfloat16, jnp.float32
    dma = pltpu.SemaphoreType.DMA
    any_space = pl.BlockSpec(memory_space=pl.ANY)
    pieces = (QUERY_CHUNKS, n, query_rows, wide)
    return pl.pallas_call(
        functools.partial(layer_kernel, n, g),
        out_shape=jax.ShapeDtypeStruct((rows, wide), bf16),
        in_specs=[any_space] * 4 + [pl.BlockSpec(memory_space=pltpu.SMEM)],
        out_specs=pl.BlockSpec(memory_space=pltpu.VMEM),
        scratch_shapes=[
            pltpu.VMEM((n, rows, wide), bf16),
            pltpu.VMEM((depth, 2 * wide), bf16),
            pltpu.VMEM(w_out.shape, bf16),
            pltpu.VMEM((rows, wide), bf16),
            pltpu.VMEM((g, rows, 2 * wide), bf16),
            pltpu.VMEM((g * rows, HD), bf16),
            pltpu.VMEM((query_rows, wide), bf16),
            pltpu.VMEM(pieces, bf16),
            pltpu.VMEM(pieces, bf16),
            pltpu.VMEM(pieces, bf16),
            pltpu.VMEM((rows, wide), f32),
            dma((4,)),
            dma((n, GATHER_CHUNKS)),
            dma((n, GATHER_CHUNKS)),
            dma((n, GATHER_CHUNKS)),
            dma((g // 2, GATHER_CHUNKS)),
            dma((g // 2, GATHER_CHUNKS)),
            dma((g, GATHER_CHUNKS)),
            dma((QUERY_CHUNKS, n)),
            dma((QUERY_CHUNKS, n)),
            dma((QUERY_CHUNKS, n)),
        ],
        compiler_params=pltpu.CompilerParams(
            collective_id=0, has_side_effects=True, vmem_limit_bytes=60 * 1024 * 1024
        ),
    )(tokens, w_query, w_value, w_out, doc_lengths)


def solution(mesh):
    return jax.shard_map(
        per_device,
        mesh=mesh,
        in_specs=(P("ctx", "head"), P(None, "head"), P(None, "head"), P("head", None), P()),
        out_specs=P("ctx", "head"),
        check_vma=False,
    )
```

time: 349 us -> 197 us (0.56)
  waiting for transfers between devices: 212 us -> 0 us
  Pallas kernels: 0 us -> 194 us
  matrix products: 86.6 us -> 0 us
  other arithmetic: 16.4 us -> 0 us
  between operations: 13.7 us -> 0.01 us
  starting transfers between devices: 10.4 us -> 0 us
  local copies, waits for them, and re-layouts: 9.52 us -> 2.26 us
    pallas_call x0 -> x1, Pallas kernels: none -> 194 us  [per_device(): pl.pallas_call(functools.partial(layer_kernel, n, g), out_shape=jax.Shape...]
    dot_general x15 -> x0, matrix products: 86.6 us -> none  [the longest x5 33.9 us: tile_weights(): jnp.einsum('qhd,khd->hqk', queries, key_rows, preferred_element_type=jnp....]
    reduce_scatter x1 -> x0, waiting for transfers between devices: 76.2 us -> none  [per_device(): lax.psum_scatter(partial_out.astype(jnp.bfloat16), 'head', scatter_dimens...]
    all_gather x1 -> x0, waiting for transfers between devices: 70.3 us -> none  [per_device(): lax.all_gather(tokens, 'head', axis=1, tiled=True)]
    ppermute x14 -> x0, waiting for transfers between devices: 64.4 us -> none  [from_behind(): return lax.ppermute(value, axis, pairs)]
    convert_element_type x2 -> x0, other arithmetic: 12.4 us -> none  [the longest x1 9.66 us: tile_weights(): return jnp.exp(scores - score_bound) * allowed.astype(jnp.float32)[None]]
    ppermute x14 -> x0, starting transfers between devices: 10.4 us -> none  [from_behind(): return lax.ppermute(value, axis, pairs)]
    slice x3 -> x0, local copies, waits for them, and re-layouts: 3.91 us -> none  [the longest x1 1.47 us: per_device(): queries = unit_heads(projected[:, :width_here], heads_here, HD)]
  transfers between devices with their start and end apart: 16 -> 0, of which waited for: 7 -> 0; matrix products, arithmetic and copies ran while one was open for 24% -> 0% of each run, Pallas kernels for 0% -> 0%
where the time goes in v1:
time: 197 us
  Pallas kernels  194 us (98%)
  local copies, waits for them, and re-layouts  2.26 us (1%)
    pallas_call x1, Pallas kernels, per_device(): pl.pallas_call(functools.partial(layer_kernel, n, g), out_shape=jax.Shape...  194 us

profile of v1, /device:TPU:0, one launch (start us, length us, event | category | flops | bytes accessed | tf_op | source)
XLA Modules:
  0.0 196.5 jit_solution(2709037283053956148)
XLA Ops:
  0.0 194.2 %shard_map.55 = bf16[1024,512]{1,0:T(8,128)(2,1)} custom-call(bf16[1024,512]{1,0:T(8,128)(2,1)} %tok_hbm.1, bf16[2048,512]{1,0:T(8,128)(2,1)} %wq_hbm.1, bf16[2048,512]{1,0:T(8,128)(2,1)} %wv_hbm.1, bf16[512,2048]{1,0:T(8,128)(2,1)} %wo_hbm.1, s32[2]{0:T(128)} %lengths.1), custom_call_target="tpu_custom_call" | custom-call | tf_op jit(solution)/shard_map/pallas_call | solution.py:305
  194.2 2.3 %copy.7 = bf16[1024,512]{1,0:T(8,128)(2,1)} copy(bf16[1024,512]{1,0:T(8,128)(2,1)} %shard_map.55) | data formatting | bytes 2097152

commit v2 on v1

--- a/solution.py
+++ b/solution.py
@@ -13,6 +13,7 @@
 EXP2_SCALE = SCORE_BOUND * math.log2(math.e)
 GATHER_CHUNKS = 8
 QUERY_CHUNKS = 4
+AHEAD = 2
 MESH = pl.DeviceIdType.MESH
 
 
@@ -111,8 +112,9 @@
             kv_copy(slot, c, partner, kv_pass.at[m, c]).start()
 
     loads[0].wait()
-    send_tok(k, 0, True)
-    send_tok(k, 0, False)
+    for c in range(AHEAD):
+        send_tok(k, c, True)
+        send_tok(k, c, False)
     ones[...] = jnp.concatenate(
         [valid_rows(block * rows, rows) for block in range(g)], axis=0
     ).astype(jnp.bfloat16)
@@ -129,10 +131,10 @@
             def _():
                 arrive(k + distance, c, False)
 
-        @pl.when(c + 1 < gather_chunks)
+        @pl.when(c + AHEAD < gather_chunks)
         def _():
-            send_tok(k, c + 1, True)
-            send_tok(k, c + 1, False)
+            send_tok(k, c + AHEAD, True)
+            send_tok(k, c + AHEAD, False)
 
         total = jnp.dot(tok[0, chunk(c)], w[0:wide], preferred_element_type=jnp.float32)
         for s in range(1, n):

time: 197 us -> 167 us (0.85)
  Pallas kernels: 194 us -> 164 us
    pallas_call x1, Pallas kernels: 194 us -> 164 us  [per_device(): pl.pallas_call(functools.partial(layer_kernel, n, g), out_shape=jax.Shape...]
where the time goes in v2:
time: 167 us
  Pallas kernels  164 us (98%)
  local copies, waits for them, and re-layouts  2.26 us (1%)
    pallas_call x1, Pallas kernels, per_device(): pl.pallas_call(functools.partial(layer_kernel, n, g), out_shape=jax.Shape...  164 us

profile of v2, /device:TPU:0, one launch (start us, length us, event | category | flops | bytes accessed | tf_op | source)
XLA Modules:
  0.0 166.6 jit_solution(14965462223487577107)
XLA Ops:
  0.0 164.3 %shard_map.55 = bf16[1024,512]{1,0:T(8,128)(2,1)} custom-call(bf16[1024,512]{1,0:T(8,128)(2,1)} %tok_hbm.1, bf16[2048,512]{1,0:T(8,128)(2,1)} %wq_hbm.1, bf16[2048,512]{1,0:T(8,128)(2,1)} %wv_hbm.1, bf16[512,2048]{1,0:T(8,128)(2,1)} %wo_hbm.1, s32[2]{0:T(128)} %lengths.1), custom_call_target="tpu_custom_call" | custom-call | tf_op jit(solution)/shard_map/pallas_call | solution.py:307
  164.3 2.3 %copy.7 = bf16[1024,512]{1,0:T(8,128)(2,1)} copy(bf16[1024,512]{1,0:T(8,128)(2,1)} %shard_map.55) | data formatting | bytes 2097152

commit v3 on v2

--- a/solution.py
+++ b/solution.py
@@ -19,13 +19,16 @@
 
 def layer_kernel(
     n, g, tok_hbm, wq_hbm, wv_hbm, wo_hbm, lengths, out_ref,
-    tok, w, wo, q, kv, ones, att, from_low, from_high, outgoing, own_sum,
+    tok, w, wo, q, kv, ones, att, from_low, from_high, outgoing, own_sum, spread, wo_own,
     load_sem, up_send, down_send, tok_recv, kv_send, kv_pass, kv_recv,
-    sum_send, low_recv, high_recv,
+    sum_send, low_recv, high_recv, spread_up, spread_down, spread_recv,
+    deal_send, share_send, wo_recv,
 ):
     rows, wide = tok_hbm.shape
     heads = wide // HD
     half = g // 2
+    ctx_count = 2 * g
+    deal_rows = wide // ctx_count
     gather_chunks, query_chunks = GATHER_CHUNKS, QUERY_CHUNKS
     step_rows = rows // gather_chunks
     query_rows = rows // query_chunks
@@ -41,6 +44,9 @@
         pltpu.make_async_copy(wq_hbm, w.at[:, pl.ds(0, wide)], load_sem.at[1]),
         pltpu.make_async_copy(wv_hbm, w.at[:, pl.ds(wide, wide)], load_sem.at[2]),
         pltpu.make_async_copy(wo_hbm, wo, load_sem.at[3]),
+        pltpu.make_async_copy(
+            wo_hbm.at[:, pl.ds(pl.multiple_of(k * wide, HD), wide)], wo_own.at[k], load_sem.at[4]
+        ),
     ]
     for load in loads:
         load.start()
@@ -50,20 +56,11 @@
     def greet(where):
         pl.semaphore_signal(barrier, inc=1, device_id=where, device_id_type=MESH)
 
-    @pl.when(k > 0)
-    def _():
-        greet({"head": k - 1})
-
-    @pl.when(k < n - 1)
-    def _():
-        greet({"head": k + 1})
-
-    greet({"ctx": base + partner})
-    for m in range(1, half):
-        greet({"ctx": base + lax.rem(j + 2 * m, g)})
-    pl.semaphore_wait(
-        barrier, jnp.where(k > 0, 1, 0) + jnp.where(k < n - 1, 1, 0) + half
-    )
+    for m in range(1, n):
+        greet({"head": lax.rem(k + m, n)})
+    for m in range(1, ctx_count):
+        greet({"ctx": lax.rem(ctx + m, ctx_count)})
+    pl.semaphore_wait(barrier, n + ctx_count - 2)
 
     limit = jnp.where(doc == 0, lengths[0], lengths[1])
 
@@ -164,6 +161,30 @@
     lax.fori_loop(0, gather_chunks, gather_step, 0)
     pass_on(gather_chunks - 1)
     loads[3].wait()
+    loads[4].wait()
+
+    def deal_copy(d):
+        mine = pl.ds(pl.multiple_of(ctx * deal_rows, deal_rows), deal_rows)
+        return pltpu.make_async_remote_copy(
+            src_ref=wo.at[mine, pl.ds(pl.multiple_of(d * wide, HD), wide)],
+            dst_ref=wo_own.at[k, mine], send_sem=deal_send.at[d], recv_sem=wo_recv.at[k, ctx],
+            device_id={"head": d}, device_id_type=MESH,
+        )
+
+    def share_copy(source, dealer, to):
+        piece = wo_own.at[
+            source, pl.ds(pl.multiple_of(dealer * deal_rows, deal_rows), deal_rows)
+        ]
+        return pltpu.make_async_remote_copy(
+            src_ref=piece, dst_ref=piece, send_sem=share_send.at[source, to],
+            recv_sem=wo_recv.at[source, dealer], device_id={"ctx": to}, device_id_type=MESH,
+        )
+
+    def other(m):
+        return lax.rem(ctx + m, ctx_count)
+
+    for m in range(1, n):
+        deal_copy(lax.rem(k + m, n)).start()
 
     def gather_end(c, carry):
         kv_copy(partner, c, partner, kv_send.at[0, c]).wait_recv()
@@ -187,7 +208,7 @@
         columns = pl.ds(pl.multiple_of(d * wide, HD), wide)
         return jnp.dot(att[...], wo[:, columns], preferred_element_type=jnp.float32)
 
-    def query_step(c, carry):
+    def attend(c, target):
         own = c * query_rows
         valid = valid_rows(j * rows + own, query_rows)
         row = lax.broadcasted_iota(jnp.int32, (query_rows, rows), 0) + own
@@ -215,51 +236,116 @@
                 )
                 total = term if total is None else total + term
             result = valid * total[:, :HD] / (total[:, HD:] + (1.0 - valid))
-            att[:, columns] = result.astype(jnp.bfloat16)
-
-        def emit(d, to, waits, landing, recv):
-            @pl.when(waits)
-            def _():
-                sum_copy(c, d, k, landing, recv).wait_recv()
-                outgoing[c, d] = (share(d) + landing[c, d].astype(jnp.float32)).astype(
-                    jnp.bfloat16
-                )
-
-            @pl.when(jnp.logical_not(waits))
-            def _():
-                outgoing[c, d] = share(d).astype(jnp.bfloat16)
-
-            sum_copy(c, d, to, landing, recv).start()
-
+            target[:, columns] = result.astype(jnp.bfloat16)
+
+    def emit(c, d, to, waits, landing, recv):
+        @pl.when(waits)
+        def _():
+            sum_copy(c, d, k, landing, recv).wait_recv()
+            outgoing[c, d] = (share(d) + landing[c, d].astype(jnp.float32)).astype(jnp.bfloat16)
+
+        @pl.when(jnp.logical_not(waits))
+        def _():
+            outgoing[c, d] = share(d).astype(jnp.bfloat16)
+
+        sum_copy(c, d, to, landing, recv).start()
+
+    def spread_copy(c, s, to, sends):
+        piece = spread.at[c, s]
+        return pltpu.make_async_remote_copy(
+            src_ref=piece, dst_ref=piece, send_sem=sends.at[c, s],
+            recv_sem=spread_recv.at[c, s], device_id={"head": to}, device_id_type=MESH,
+        )
+
+    def relay(c, distance):
+        @pl.when(jnp.logical_and(k - distance >= 0, k < n - 1))
+        def _():
+            spread_copy(c, k - distance, k, spread_up).wait_recv()
+            spread_copy(c, k - distance, k + 1, spread_up).start()
+
+        @pl.when(jnp.logical_and(k + distance < n, k > 0))
+        def _():
+            spread_copy(c, k + distance, k, spread_down).wait_recv()
+            spread_copy(c, k + distance, k - 1, spread_down).start()
+
+    def pair_step(c, carry):
+        attend(2 * c, spread.at[c, k])
+
+        @pl.when(k < n - 1)
+        def _():
+            spread_copy(c, k, k + 1, spread_up).start()
+
+        @pl.when(k > 0)
+        def _():
+            spread_copy(c, k, k - 1, spread_down).start()
+
+        @pl.when(c == 0)
+        def _():
+            for m in range(1, n):
+                source = lax.rem(k + m, n)
+                share_copy(source, ctx, ctx).wait_recv()
+
+                def hand_out(step, inner):
+                    share_copy(source, ctx, other(step)).start()
+                    return inner
+
+                lax.fori_loop(1, ctx_count, hand_out, 0)
+
+        attend(2 * c + 1, att)
+        relay(c, 1)
         for off in range(n - 1, 0, -1):
             @pl.when(k + off < n)
             def _():
-                emit(k + off, k + 1, k > 0, from_low, low_recv)
+                emit(c, k + off, k + 1, k > 0, from_low, low_recv)
 
             @pl.when(k - off >= 0)
             def _():
-                emit(k - off, k - 1, k < n - 1, from_high, high_recv)
-
-        own_sum[query_chunk(c)] = share(k)
-        return carry
-
-    lax.fori_loop(0, query_chunks, query_step, 0)
+                emit(c, k - off, k - 1, k < n - 1, from_high, high_recv)
+
+        own_sum[c] = share(k)
+        for distance in range(2, n):
+            relay(c, distance)
+        return carry
+
+    pairs = query_chunks // 2
+    lax.fori_loop(0, pairs, pair_step, 0)
+
+    def collect(step, carry):
+        for m in range(1, n):
+            share_copy(lax.rem(k + m, n), other(step), ctx).wait_recv()
+        return carry
+
+    lax.fori_loop(1, ctx_count, collect, 0)
 
     def finish(c, carry):
+        for distance in range(1, n):
+            @pl.when(jnp.logical_and(k - distance >= 0, k == n - 1))
+            def _():
+                spread_copy(c, k - distance, k, spread_up).wait_recv()
+
+            @pl.when(jnp.logical_and(k + distance < n, k == 0))
+            def _():
+                spread_copy(c, k + distance, k, spread_down).wait_recv()
+
+        total = jnp.dot(spread[c, 0], wo_own[0], preferred_element_type=jnp.float32)
+        for s in range(1, n):
+            total += jnp.dot(spread[c, s], wo_own[s], preferred_element_type=jnp.float32)
+        out_ref[query_chunk(2 * c)] = total.astype(out_ref.dtype)
+
         @pl.when(k > 0)
         def _():
             sum_copy(c, k, k, from_low, low_recv).wait_recv()
-            own_sum[query_chunk(c)] += from_low[c, k].astype(jnp.float32)
+            own_sum[c] += from_low[c, k].astype(jnp.float32)
 
         @pl.when(k < n - 1)
         def _():
             sum_copy(c, k, k, from_high, high_recv).wait_recv()
-            own_sum[query_chunk(c)] += from_high[c, k].astype(jnp.float32)
-
-        out_ref[query_chunk(c)] = own_sum[query_chunk(c)].astype(out_ref.dtype)
-        return carry
-
-    lax.fori_loop(0, query_chunks, finish, 0)
+            own_sum[c] += from_high[c, k].astype(jnp.float32)
+
+        out_ref[query_chunk(2 * c + 1)] = own_sum[c].astype(out_ref.dtype)
+        return carry
+
+    lax.fori_loop(0, pairs, finish, 0)
 
     def drain_gather(c, carry):
         for s in range(n):
@@ -289,9 +375,26 @@
             def _():
                 sum_copy(c, d, k - 1, from_high, high_recv).wait_send()
 
-        return carry
-
-    lax.fori_loop(0, query_chunks, drain_sums, 0)
+            @pl.when(jnp.logical_and(d <= k, k < n - 1))
+            def _():
+                spread_copy(c, d, k + 1, spread_up).wait_send()
+
+            @pl.when(jnp.logical_and(d >= k, k > 0))
+            def _():
+                spread_copy(c, d, k - 1, spread_down).wait_send()
+
+        return carry
+
+    lax.fori_loop(0, pairs, drain_sums, 0)
+    for m in range(1, n):
+        deal_copy(lax.rem(k + m, n)).wait_send()
+
+    def drain_shares(step, carry):
+        for m in range(1, n):
+            share_copy(lax.rem(k + m, n), ctx, other(step)).wait_send()
+        return carry
+
+    lax.fori_loop(1, ctx_count, drain_shares, 0)
 
 
 def per_device(tokens, w_query, w_value, w_out, doc_lengths):
@@ -303,7 +406,8 @@
     bf16, f32 = jnp.bfloat16, jnp.float32
     dma = pltpu.SemaphoreType.DMA
     any_space = pl.BlockSpec(memory_space=pl.ANY)
-    pieces = (QUERY_CHUNKS, n, query_rows, wide)
+    pairs = QUERY_CHUNKS // 2
+    pieces = (pairs, n, query_rows, wide)
     return pl.pallas_call(
         functools.partial(layer_kernel, n, g),
         out_shape=jax.ShapeDtypeStruct((rows, wide), bf16),
@@ -320,17 +424,25 @@
             pltpu.VMEM(pieces, bf16),
             pltpu.VMEM(pieces, bf16),
             pltpu.VMEM(pieces, bf16),
-            pltpu.VMEM((rows, wide), f32),
-            dma((4,)),
+            pltpu.VMEM((pairs, query_rows, wide), f32),
+            pltpu.VMEM(pieces, bf16),
+            pltpu.VMEM((n, wide, wide), bf16),
+            dma((5,)),
             dma((n, GATHER_CHUNKS)),
             dma((n, GATHER_CHUNKS)),
             dma((n, GATHER_CHUNKS)),
             dma((g // 2, GATHER_CHUNKS)),
             dma((g // 2, GATHER_CHUNKS)),
             dma((g, GATHER_CHUNKS)),
-            dma((QUERY_CHUNKS, n)),
-            dma((QUERY_CHUNKS, n)),
-            dma((QUERY_CHUNKS, n)),
+            dma((pairs, n)),
+            dma((pairs, n)),
+            dma((pairs, n)),
+            dma((pairs, n)),
+            dma((pairs, n)),
+            dma((pairs, n)),
+            dma((n,)),
+            dma((n, 2 * g)),
+            dma((n, 2 * g)),
         ],
         compiler_params=pltpu.CompilerParams(
             collective_id=0, has_side_effects=True, vmem_limit_bytes=60 * 1024 * 1024

time: 167 us -> 155 us (0.928)
  Pallas kernels: 164 us -> 151 us
    pallas_call x1, Pallas kernels: 164 us -> 151 us  [per_device(): pl.pallas_call(functools.partial(layer_kernel, n, g), out_shape=jax.Shape...]
where the time goes in v3:
time: 155 us; the launch traced here: 154 us
  Pallas kernels  151 us (97%)
  local copies, waits for them, and re-layouts  2.26 us (1%)
    pallas_call x1, Pallas kernels, per_device(): pl.pallas_call(functools.partial(layer_kernel, n, g), out_shape=jax.Shape...  151 us

profile of v3, /device:TPU:0, one launch (start us, length us, event | category | flops | bytes accessed | tf_op | source)
XLA Modules:
  0.0 153.5 jit_solution(11774350785811851212)
XLA Ops:
  0.0 151.2 %shard_map.55 = bf16[1024,512]{1,0:T(8,128)(2,1)} custom-call(bf16[1024,512]{1,0:T(8,128)(2,1)} %tok_hbm.1, bf16[2048,512]{1,0:T(8,128)(2,1)} %wq_hbm.1, bf16[2048,512]{1,0:T(8,128)(2,1)} %wv_hbm.1, bf16[512,2048]{1,0:T(8,128)(2,1)} %wo_hbm.1, s32[2]{0:T(128)} %lengths.1), custom_call_target="tpu_custom_call" | custom-call | tf_op jit(solution)/shard_map/pallas_call | solution.py:411
  151.2 2.3 %copy.7 = bf16[1024,512]{1,0:T(8,128)(2,1)} copy(bf16[1024,512]{1,0:T(8,128)(2,1)} %shard_map.55) | data formatting | bytes 2097152

commit v4 on v3

--- a/solution.py
+++ b/solution.py
@@ -19,7 +19,7 @@
 
 def layer_kernel(
     n, g, tok_hbm, wq_hbm, wv_hbm, wo_hbm, lengths, out_ref,
-    tok, w, wo, q, kv, ones, att, from_low, from_high, outgoing, own_sum, spread, wo_own,
+    tok, w, wo, q, kv, ones, att, from_low, from_high, outgoing, own_sum, spread, wo_own, projected, mixed,
     load_sem, up_send, down_send, tok_recv, kv_send, kv_pass, kv_recv,
     sum_send, low_recv, high_recv, spread_up, spread_down, spread_recv,
     deal_send, share_send, wo_recv,
@@ -119,6 +119,11 @@
     loads[2].wait()
 
     def gather_step(c, carry):
+        def product(source):
+            depth = pl.ds(pl.multiple_of(source * wide, HD), wide)
+            return jnp.dot(tok[source, chunk(c)], w[depth], preferred_element_type=jnp.float32)
+
+        projected[...] = product(k)
         for distance in range(1, n):
             @pl.when(k - distance >= 0)
             def _():
@@ -128,17 +133,20 @@
             def _():
                 arrive(k + distance, c, False)
 
+            @pl.when(k - distance >= 0)
+            def _():
+                projected[...] += product(k - distance)
+
+            @pl.when(k + distance < n)
+            def _():
+                projected[...] += product(k + distance)
+
         @pl.when(c + AHEAD < gather_chunks)
         def _():
             send_tok(k, c + AHEAD, True)
             send_tok(k, c + AHEAD, False)
 
-        total = jnp.dot(tok[0, chunk(c)], w[0:wide], preferred_element_type=jnp.float32)
-        for s in range(1, n):
-            total += jnp.dot(
-                tok[s, chunk(c)], w[s * wide:(s + 1) * wide],
-                preferred_element_type=jnp.float32,
-            )
+        total = projected[...]
         valid = valid_rows(j * rows + c * step_rows, step_rows)
         for h in range(heads):
             columns = slice(h * HD, (h + 1) * HD)
@@ -159,7 +167,6 @@
         return carry
 
     lax.fori_loop(0, gather_chunks, gather_step, 0)
-    pass_on(gather_chunks - 1)
     loads[3].wait()
     loads[4].wait()
 
@@ -186,14 +193,16 @@
     for m in range(1, n):
         deal_copy(lax.rem(k + m, n)).start()
 
-    def gather_end(c, carry):
-        kv_copy(partner, c, partner, kv_send.at[0, c]).wait_recv()
-        for m in range(1, half):
-            slot = lax.rem(partner + g - 2 * m, g)
-            kv_copy(slot, c, partner, kv_pass.at[m, c]).wait_recv()
-        return carry
-
-    lax.fori_loop(0, gather_chunks, gather_end, 0)
+    def settle(slot):
+        def landed(c, carry):
+            kv_copy(slot, c, partner, kv_send.at[0, c]).wait_recv()
+            return carry
+
+        lax.fori_loop(0, gather_chunks, landed, 0)
+
+    blocks = [j, partner]
+    blocks += [behind(m) for m in range(1, half)]
+    blocks += [lax.rem(partner + g - 2 * m, g) for m in range(1, half)]
 
     def sum_copy(c, d, to, landing, recv):
         return pltpu.make_async_remote_copy(
@@ -213,30 +222,40 @@
         valid = valid_rows(j * rows + own, query_rows)
         row = lax.broadcasted_iota(jnp.int32, (query_rows, rows), 0) + own
         column = lax.broadcasted_iota(jnp.int32, (query_rows, rows), 1)
-        for h in range(heads):
-            columns = slice(h * HD, (h + 1) * HD)
-            shifted = slice(wide + h * HD, wide + (h + 1) * HD)
-            queries = q[query_chunk(c), columns]
-            total = None
-            for b in range(g):
-                block = lax.rem(j + b, g)
+        for b, block in enumerate(blocks):
+            if b == 1 or b > half:
+                @pl.when(c == 0)
+                def _():
+                    settle(block)
+            if b == 2:
+                @pl.when(c == 0)
+                def _():
+                    pass_on(gather_chunks - 1)
+
+            block_rows = pl.ds(pl.multiple_of(block * rows, rows), rows)
+            for h in range(heads):
+                columns = slice(h * HD, (h + 1) * HD)
+                shifted = slice(wide + h * HD, wide + (h + 1) * HD)
                 scores = lax.dot_general(
-                    queries, kv[block, :, columns], (((1,), (1,)), ((), ())),
-                    preferred_element_type=jnp.float32,
+                    q[query_chunk(c), columns], kv[block, :, columns],
+                    (((1,), (1,)), ((), ())), preferred_element_type=jnp.float32,
                 )
                 weights = jnp.exp2(scores)
                 if b == 0:
                     weights = jnp.where(row != column, weights, 0.0)
-                block_rows = pl.ds(pl.multiple_of(block * rows, rows), rows)
                 values = jnp.concatenate(
                     [kv[block, :, shifted], ones[block_rows]], axis=1
                 )
                 term = jnp.dot(
                     weights.astype(jnp.bfloat16), values, preferred_element_type=jnp.float32
                 )
-                total = term if total is None else total + term
-            result = valid * total[:, :HD] / (total[:, HD:] + (1.0 - valid))
-            target[:, columns] = result.astype(jnp.bfloat16)
+                if b == 0:
+                    mixed[h] = term
+                else:
+                    mixed[h] += term
+        for h in range(heads):
+            result = valid * mixed[h, :, :HD] / (mixed[h, :, HD:] + (1.0 - valid))
+            target[:, h * HD:(h + 1) * HD] = result.astype(jnp.bfloat16)
 
     def emit(c, d, to, waits, landing, recv):
         @pl.when(waits)
@@ -427,6 +446,8 @@
             pltpu.VMEM((pairs, query_rows, wide), f32),
             pltpu.VMEM(pieces, bf16),
             pltpu.VMEM((n, wide, wide), bf16),
+            pltpu.VMEM((rows // GATHER_CHUNKS, 2 * wide), f32),
+            pltpu.VMEM((wide // HD, query_rows, 2 * HD), f32),
             dma((5,)),
             dma((n, GATHER_CHUNKS)),
             dma((n, GATHER_CHUNKS)),

time: 155 us -> 150 us (0.968)
  Pallas kernels: 151 us -> 148 us
    pallas_call x1, Pallas kernels: 151 us -> 148 us  [per_device(): pl.pallas_call(functools.partial(layer_kernel, n, g), out_shape=jax.Shape...]
where the time goes in v4:
time: 150 us
  Pallas kernels  148 us (99%)
  local copies, waits for them, and re-layouts  2.26 us (2%)
    pallas_call x1, Pallas kernels, per_device(): pl.pallas_call(functools.partial(layer_kernel, n, g), out_shape=jax.Shape...  148 us

profile of v4, /device:TPU:0, one launch (start us, length us, event | category | flops | bytes accessed | tf_op | source)
XLA Modules:
  0.0 149.9 jit_solution(17580916063822670129)
XLA Ops:
  0.0 147.6 %shard_map.55 = bf16[1024,512]{1,0:T(8,128)(2,1)} custom-call(bf16[1024,512]{1,0:T(8,128)(2,1)} %tok_hbm.1, bf16[2048,512]{1,0:T(8,128)(2,1)} %wq_hbm.1, bf16[2048,512]{1,0:T(8,128)(2,1)} %wv_hbm.1, bf16[512,2048]{1,0:T(8,128)(2,1)} %wo_hbm.1, s32[2]{0:T(128)} %lengths.1), custom_call_target="tpu_custom_call" | custom-call | tf_op jit(solution)/shard_map/pallas_call | solution.py:430
  147.6 2.3 %copy.7 = bf16[1024,512]{1,0:T(8,128)(2,1)} copy(bf16[1024,512]{1,0:T(8,128)(2,1)} %shard_map.55) | data formatting | bytes 2097152

commit v5 on v4

--- a/solution.py
+++ b/solution.py
@@ -12,7 +12,7 @@
 SCORE_BOUND = 24.0
 EXP2_SCALE = SCORE_BOUND * math.log2(math.e)
 GATHER_CHUNKS = 8
-QUERY_CHUNKS = 4
+QUERY_CHUNKS = 8
 AHEAD = 2
 MESH = pl.DeviceIdType.MESH
 

time: 150 us -> 154 us (1.027)
  Pallas kernels: 148 us -> 151 us
    pallas_call x1, Pallas kernels: 148 us -> 151 us  [per_device(): pl.pallas_call(functools.partial(layer_kernel, n, g), out_shape=jax.Shape...]
where the time goes in v5:
time: 154 us
  Pallas kernels  151 us (98%)
  local copies, waits for them, and re-layouts  2.26 us (1%)
    pallas_call x1, Pallas kernels, per_device(): pl.pallas_call(functools.partial(layer_kernel, n, g), out_shape=jax.Shape...  151 us

profile of v5, /device:TPU:0, one launch (start us, length us, event | category | flops | bytes accessed | tf_op | source)
XLA Modules:
  0.0 153.7 jit_solution(3102910508511442911)
XLA Ops:
  0.0 151.4 %shard_map.55 = bf16[1024,512]{1,0:T(8,128)(2,1)} custom-call(bf16[1024,512]{1,0:T(8,128)(2,1)} %tok_hbm.1, bf16[2048,512]{1,0:T(8,128)(2,1)} %wq_hbm.1, bf16[2048,512]{1,0:T(8,128)(2,1)} %wv_hbm.1, bf16[512,2048]{1,0:T(8,128)(2,1)} %wo_hbm.1, s32[2]{0:T(128)} %lengths.1), custom_call_target="tpu_custom_call" | custom-call | tf_op jit(solution)/shard_map/pallas_call | solution.py:430
  151.4 2.3 %copy.7 = bf16[1024,512]{1,0:T(8,128)(2,1)} copy(bf16[1024,512]{1,0:T(8,128)(2,1)} %shard_map.55) | data formatting | bytes 2097152
